TPU v7x, 32 devices: a whole 2x2x4 slice. The times are simulated.
32 devices in a mesh: groups: 2 (over x), seq: 16 (over z, y, core).
Axes of the slice: x: 2, y: 2, z: 4, core: 2. Of those that a mesh axis runs over, the one named last changes fastest.
Arguments:
- query_vals: bfloat16 [24576, 2048], P(('groups', 'seq')), parts along dimension 0, may hold values from -6 to 6
- query_scale: float32 [192, 16], P(('groups', 'seq')), parts along dimension 0, may hold values from 0.6 to 1.6
- key_vals: bfloat16 [24576, 2048], P(('groups', 'seq')), parts along dimension 0, may hold values from -8 to 8
- key_scale: float32 [192, 16], P(('groups', 'seq')), parts along dimension 0, may hold values from 0.6 to 1.6
- value_vals: bfloat16 [24576, 2048], P(('groups', 'seq')), parts along dimension 0, may hold values from -8 to 8
- value_scale: float32 [192, 16], P(('groups', 'seq')), parts along dimension 0, may hold values from 0.6 to 1.6
- feature_matrix: bfloat16 [128, 256], replicated, may hold values from -5 to 5
- cotangent: bfloat16 [24576, 2048], P(('groups', 'seq')), parts along dimension 0, may hold values from -6 to 6
Outputs:
- attended: bfloat16 [24576, 2048], P(('groups', 'seq')), parts along dimension 0
- query_grad: bfloat16 [24576, 2048], P(('groups', 'seq')), parts along dimension 0
- key_grad: bfloat16 [24576, 2048], P(('groups', 'seq')), parts along dimension 0
- value_grad: bfloat16 [24576, 2048], P(('groups', 'seq')), parts along dimension 0
There are 2 independent parts, one for each index of `groups`. A program takes and returns all parts, laid end to end along the dimension named above; an argument that names none is the same for every part. Nothing has to cross between parts.
All inputs are finite; a program needn't handle non-finite values.
Results may differ from a plain program's by a relative error of at most 0.025.
Values sent between devices are 32-bit elements; how exact they have to be, the bound alone decides.
A program may use at most 128 MiB of HBM per device.

v0:
```python
import jax
import jax.numpy as jnp
from jax import lax
from jax.sharding import PartitionSpec as P


def spread_scale(scale, count):
    blocks = scale.shape[0]
    return jnp.broadcast_to(scale[:, None, :], (blocks, count // blocks, scale.shape[1])).reshape(
        count, scale.shape[1]
    )


def per_device(
    query_vals, query_scale, key_vals, key_scale, value_vals, value_scale, feature_matrix, cotangent
):
    count = query_vals.shape[0]
    head_count = query_scale.shape[1]
    head_width = feature_matrix.shape[0]
    root_four = head_width**0.25
    root_two = head_width**0.5
    query_rows = query_vals.reshape(count, head_count, head_width)
    key_rows = key_vals.reshape(count, head_count, head_width)
    value_rows = value_vals.reshape(count, head_count, head_width)
    upstream = cotangent.reshape(count, head_count, head_width)
    query_factor = spread_scale(query_scale, count)
    key_factor = spread_scale(key_scale, count)
    value_factor = spread_scale(value_scale, count)
    key_float = key_rows.astype(jnp.float32) * key_factor[:, :, None]
    key_proj = (
        jnp.einsum("thd,dm->thm", key_rows, feature_matrix, preferred_element_type=jnp.float32)
        * (key_factor / root_four)[:, :, None]
    )
    key_proj = key_proj - (jnp.sum(key_float * key_float, axis=2) / (2.0 * root_two))[:, :, None]
    key_random_features = jnp.exp(key_proj).astype(jnp.bfloat16)
    block_value = (value_rows.astype(jnp.float32) * value_factor[:, :, None]).astype(jnp.bfloat16)
    partial_state = jnp.einsum(
        "nge,ngs->ges", key_random_features, block_value, preferred_element_type=jnp.float32
    )
    norm_part = jnp.sum(key_random_features.astype(jnp.float32), axis=0)
    query_proj = (
        jnp.einsum("thd,dm->thm", query_rows, feature_matrix, preferred_element_type=jnp.float32)
        * (query_factor / root_four)[:, :, None]
    )
    query_random_features = jnp.exp(query_proj).astype(jnp.bfloat16)
    query_float = query_random_features.astype(jnp.float32)
    state, normalizer = lax.psum((partial_state, norm_part), "seq")
    total = jnp.sum(normalizer, axis=1)
    denominator = jnp.einsum("thm,hm->th", query_float, normalizer, precision=lax.Precision.HIGHEST)
    scaled = upstream.astype(jnp.float32) / denominator[:, :, None]
    scaled_block = scaled.astype(jnp.bfloat16)
    block_state = (state / total[:, None, None]).astype(jnp.bfloat16)
    attention_numerator = jnp.einsum(
        "wkz,kzl->wkl", query_random_features, block_state, preferred_element_type=jnp.float32
    )
    attended_f = attention_numerator * (total[None, :] / denominator)[:, :, None]
    coupling = jnp.sum(scaled * attended_f, axis=2)
    partial_gradient = jnp.einsum(
        "nge,ngs->ges", query_random_features, scaled_block, preferred_element_type=jnp.float32
    )
    norm_grad_part = -jnp.einsum(
        "thm,th->hm", query_float, coupling, precision=lax.Precision.HIGHEST
    )
    state_grad, normalizer_grad = lax.psum((partial_gradient, norm_grad_part), "seq")
    block_state_gradient = (state_grad * total[:, None, None]).astype(jnp.bfloat16)
    query_phi_grad = (
        total[None, :, None]
        * jnp.einsum("vcs,cus->vcu", scaled_block, block_state, preferred_element_type=jnp.float32)
        - coupling[:, :, None] * normalizer[None, :, :]
    )
    query_proj_grad = (query_phi_grad * query_float).astype(jnp.bfloat16)
    query_grad = (
        jnp.einsum(
            "thm,dm->thd", query_proj_grad, feature_matrix, preferred_element_type=jnp.float32
        )
        / root_four
    )
    key_phi_grad = (
        jnp.einsum(
            "vcs,cus->vcu", block_value, block_state_gradient, preferred_element_type=jnp.float32
        )
        / total[None, :, None]
        + normalizer_grad[None, :, :]
    )
    key_proj_grad = key_phi_grad * key_random_features.astype(jnp.float32)
    key_grad = (
        jnp.einsum(
            "thm,dm->thd",
            key_proj_grad.astype(jnp.bfloat16),
            feature_matrix,
            preferred_element_type=jnp.float32,
        )
        / root_four
    )
    key_grad = key_grad - jnp.sum(key_proj_grad, axis=2)[:, :, None] * key_float / root_two
    value_grad = (
        jnp.einsum(
            "wkz,kzl->wkl",
            key_random_features,
            block_state_gradient,
            preferred_element_type=jnp.float32,
        )
        / total[None, :, None]
    )
    flat_width = head_count * head_width
    return (
        attended_f.astype(jnp.bfloat16).reshape(count, flat_width),
        query_grad.astype(jnp.bfloat16).reshape(count, flat_width),
        key_grad.astype(jnp.bfloat16).reshape(count, flat_width),
        value_grad.astype(jnp.bfloat16).reshape(count, flat_width),
    )


def solution(mesh):
    in_specs = (
        P(("groups", "seq"), None),
        P(("groups", "seq"), None),
        P(("groups", "seq"), None),
        P(("groups", "seq"), None),
        P(("groups", "seq"), None),
        P(("groups", "seq"), None),
        P(),
        P(("groups", "seq"), None),
    )
    out_specs = (
        P(("groups", "seq"), None),
        P(("groups", "seq"), None),
        P(("groups", "seq"), None),
        P(("groups", "seq"), None),
    )
    return jax.shard_map(
        per_device, mesh=mesh, in_specs=in_specs, out_specs=out_specs, check_vma=False
    )
```

profile of v0, /device:TPU:0, one launch (start us, length us, event | category | flops | bytes accessed | tf_op | source)
XLA Modules:
  0.0 347.1 jit_solution(10090545493286488750)
XLA Ops:
  7.2 0.9 copy.32
  8.3 4.6 %copy.30 = bf16[768,2048]{0,1:T(8,128)(2,1)} copy(bf16[768,2048]{1,0:T(8,128)(2,1)} %param.10) | data formatting | bytes 6291456 | tf_op args[2]
  12.9 2.8 multiply_reduce_fusion.1
  15.7 7.4 %convert_reduce_fusion = (f32[16,256]{1,0:T(8,128)S(1)}, bf16[768,16,256]{2,0,1:T(8,128)(2,1)}) fusion(f32[768,16]{0,1:T(8,128)S(1)} %broadcast_multiply_fusion, f32[768,16]{0,1:T(8,128)S(1)} %get-tuple-element.14, bf16[768,16,128]{0,2,1:T(8,128)(2,1)} %bitcast.96, bf16[128,256]{1,0:T(8,128)(2,1)S(1)} %copy-done.11), kind=kOutput, calls=%fused_computation.1 | convolution fusion | flops 821030912 | bytes 9617408 | tf_op jit(solution)/shard_map/thd,dm->thm/dot_general | solution.py:31
  23.2 62.9 %psum.29 = f32[16,256]{1,0:T(8,128)S(1)} all-reduce(f32[16,256]{1,0:T(8,128)S(1)} %get-tuple-element.18), channel_id=1, replica_groups=mesh['groups'=2,'seq'=16] {'seq'}, use_global_device_ids=true, to_apply=%region_3.0 | all-reduce | flops 4096 | bytes 32768 | tf_op jit(solution)/shard_map/psum | solution.py:47
  86.3 3.0 exponential_convert_fusion
  89.4 3.2 copy-done.2
  92.5 5.0 %fusion.29 = f32[16,1,768]{2,1,0:T(1,128)S(1)} fusion(bf16[768,16,256]{2,0,1:T(8,128)(2,1)S(1)} %exponential_convert_fusion, f32[16,256,1]{1,0,2:T(8,128)S(1)} %bitcast.107), kind=kOutput, calls=%fused_computation.46 | convolution fusion | flops 37748736 | bytes 6356992 | tf_op jit(solution)/shard_map/thm,hm->th/dot_general | solution.py:49
  97.5 3.6 %copy.39 = f32[768,2048]{0,1:T(8,128)} copy(bf16[768,2048]{1,0:T(8,128)(2,1)S(1)} %copy-done.4) | data formatting | bytes 9437184 | tf_op jit(solution)/shard_map/convert_element_type | solution.py:50
  101.3 8.1 %fusion.32 = f32[16,256,128]{2,1,0:T(8,128)} fusion(bf16[768,16,256]{2,0,1:T(8,128)(2,1)} %copy-done.2, f32[768,16,128]{0,2,1:T(8,128)} %bitcast.98, f32[768,16]{0,1:T(8,128)S(1)} %bitcast.112), kind=kOutput, calls=%fused_computation.50 | convolution fusion | flops 808452096 | bytes 14729216 | tf_op jit(solution)/shard_map/nge,ngs->ges/dot_general | solution.py:58
  109.4 6.7 %fusion.21 = f32[16,256,128]{2,1,0:T(8,128)} fusion(bf16[768,16,256]{2,0,1:T(8,128)(2,1)} %get-tuple-element.19, f32[768,16]{0,1:T(8,128)S(1)} %bitcast.109, bf16[768,2048]{1,0:T(8,128)(2,1)S(1)} %copy-done.7), kind=kOutput, calls=%fused_computation.31 | convolution fusion | flops 810024960 | bytes 11583488 | tf_op jit(solution)/shard_map/nge,ngs->ges/dot_general | solution.py:37
  116.1 0.1 reduce_sum.47
  116.3 109.1 %all-reduce.3.cloned.1.call-done = (f32[16,256,128]{2,1,0:T(8,128)}, f32[16,256,128]{2,1,0:T(8,128)}) async-done(((f32[16,256,128]{2,1,0:T(8,128)}, f32[16,256,128]{2,1,0:T(8,128)}), (f32[16,256,128]{2,1,0:T(8,128)}, f32[16,256,128]{2,1,0:T(8,128)})) %all-reduce.3.cloned.1.call-update) | async-done | bytes 4194320 | tf_op jit(solution)/shard_map/psum | solution.py:47
  225.4 7.9 %multiply_reduce_fusion = (f32[768,16]{0,1:T(8,128)S(1)}, bf16[768,16,128]{0,2,1:T(8,128)(2,1)S(1)}) fusion(f32[768,16]{0,1:T(8,128)S(1)} %broadcast_divide_fusion.1, f32[768,16]{0,1:T(8,128)S(1)} %bitcast.113, f32[768,2048]{0,1:T(8,128)} %copy.39, bf16[768,16,256]{2,0,1:T(8,128)(2,1)} %copy-done.2, f32[16,256,128]{2,1,0:T(8,128)} %get-tuple-element.12, ...), kind=kOutput, calls=%fused_computation.19 | convolution fusion | flops 814206976 | bytes 17973312 | tf_op jit(solution)/shard_map/wkz,kzl->wkl/dot_general | solution.py:53
  233.3 2.9 copy.44
  236.2 8.7 %multiply_convert_fusion = bf16[768,16,128]{0,2,1:T(8,128)(2,1)S(1)} fusion(bf16[768,16,256]{2,0,1:T(8,128)(2,1)} %copy-done.2, f32[16,256]{1,0:T(8,128)S(1)} %psum.29, f32[768,16]{0,1:T(8,128)S(1)} %get-tuple-element.16, f32[16]{0:T(128)S(1)} %reduce_sum.47, bf16[128,256]{1,0:T(8,128)(2,1)S(1)} %copy-done.11, f32[16,256,128]{2,1,0:T(8,128)} %get-tuple-element.12, ...), kind=kOutput, calls=%fused_computation.16 | convolution fusion | flops 1636827136 | bytes 18006080 | tf_op jit(solution)/shard_map/thm,dm->thd/dot_general | solution.py:73
  245.0 2.9 copy.45
  247.8 5.5 %fusion.27 = f32[16,1,256]{2,1,0:T(1,128)S(1)} fusion(bf16[768,16,256]{2,0,1:T(8,128)(2,1)} %copy-done.2, f32[768,16,1]{0,1,2:T(8,128)S(1)} %bitcast.108), kind=kOutput, calls=%fused_computation.39 | convolution fusion | flops 37748736 | bytes 6356992 | tf_op jit(solution)/shard_map/thm,th->hm/dot_general | solution.py:61
  253.3 59.4 %psum.31 = f32[16,256]{1,0:T(8,128)S(1)} all-reduce(f32[16,256]{1,0:T(8,128)S(1)} %bitcast_negate_fusion), channel_id=1, replica_groups=mesh['groups'=2,'seq'=16] {'seq'}, use_global_device_ids=true, to_apply=%region_7.0 | all-reduce | flops 4096 | bytes 32768 | tf_op jit(solution)/shard_map/psum | solution.py:64
  312.8 7.5 %divide_convert_fusion = bf16[16,128,768]{2,1,0:T(8,128)(2,1)} fusion(f32[16]{0:T(128)S(1)} %reduce_sum.47, bf16[768,16,256]{2,0,1:T(8,128)(2,1)} %get-tuple-element.19, f32[16,256,128]{2,1,0:T(8,128)S(1)} %copy-done.9), kind=kOutput, calls=%fused_computation.12 | convolution fusion | flops 809500672 | bytes 11534400 | tf_op jit(solution)/shard_map/wkz,kzl->wkl/dot_general | solution.py:97
  320.2 6.6 %fusion.36 = (f32[768,16]{0,1:T(8,128)S(1)}, bf16[768,16,256]{2,0,1:T(8,128)(2,1)S(1)}) fusion(bf16[768,16,256]{2,0,1:T(8,128)(2,1)} %get-tuple-element.19, f32[16,256]{1,0:T(8,128)S(1)} %psum.31, f32[16]{0:T(128)S(1)} %reduce_sum.47, f32[768,16]{0,1:T(8,128)S(1)} %bitcast.110, f32[16,256,128]{2,1,0:T(8,128)S(1)} %copy-done.10, ...), kind=kOutput, calls=%fused_computation.51 | convolution fusion | flops 829935616 | bytes 17940544 | tf_op jit(solution)/shard_map/vcs,cus->vcu/dot_general | solution.py:79
  326.8 4.1 %subtract_convert_fusion = bf16[768,16,128]{0,2,1:T(8,128)(2,1)} fusion(bf16[768,16,128]{0,2,1:T(8,128)(2,1)S(1)} %bitcast.97, f32[768,16]{0,1:T(8,128)S(1)} %get-tuple-element.20, f32[768,16]{0,1:T(8,128)S(1)} %get-tuple-element.15, bf16[768,16,256]{2,0,1:T(8,128)(2,1)S(1)} %get-tuple-element.21, bf16[128,256]{1,0:T(8,128)(2,1)S(1)} %copy-done.11), kind=kOutput, calls=%fused_computation.13 | convolution fusion | flops 816316416 | bytes 12746752 | tf_op jit(solution)/shard_map/thm,dm->thd/dot_general | solution.py:87
  330.9 4.8 %copy.46 = bf16[768,2048]{1,0:T(8,128)(2,1)} copy(bf16[768,2048]{0,1:T(8,128)(2,1)} %bitcast.102) | data formatting | bytes 6291456
  335.7 4.6 %copy.47 = bf16[768,2048]{1,0:T(8,128)(2,1)} copy(bf16[768,2048]{0,1:T(8,128)(2,1)} %bitcast.100) | data formatting | bytes 6291456
  (38 shorter events, 0.7 us)
Async XLA Ops:
  7.2 79.1 %copy-start = (bf16[768,2048]{1,0:T(8,128)(2,1)S(1)}, bf16[768,2048]{1,0:T(8,128)(2,1)}, u32[]{:S(2)}) copy-start(bf16[768,2048]{1,0:T(8,128)(2,1)} %param.8) | copy-start | bytes 9437188
  7.2 8.5 %copy-start.11 = (bf16[128,256]{1,0:T(8,128)(2,1)S(1)}, bf16[128,256]{1,0:T(8,128)(2,1)}, u32[]{:S(2)}) copy-start(bf16[128,256]{1,0:T(8,128)(2,1)} %param.14) | copy-start | bytes 196612
  7.2 218.2 %all-reduce.3.cloned.1.call-start = ((), (), s32[]{:S(2)}) async-start(), calls=%async_computation | async-start | bytes 8388608 | tf_op jit(solution)/shard_map/psum | solution.py:47
  15.7 70.4 %copy-start.6 = (f32[6,16]{1,0:T(8,128)S(1)}, f32[6,16]{1,0:T(8,128)}, u32[]{:S(2)}) copy-start(f32[6,16]{1,0:T(8,128)} %param.9) | copy-start | bytes 1156
  89.3 3.2 copy-start.2
  89.3 8.2 %copy-start.4 = (bf16[768,2048]{1,0:T(8,128)(2,1)S(1)}, bf16[768,2048]{1,0:T(8,128)(2,1)}, u32[]{:S(2)}) copy-start(bf16[768,2048]{1,0:T(8,128)(2,1)} %param.15) | copy-start | bytes 9437188
  97.5 3.6 %copy-start.5 = (f32[6,16]{1,0:T(8,128)S(1)}, f32[6,16]{1,0:T(8,128)}, u32[]{:S(2)}) copy-start(f32[6,16]{1,0:T(8,128)} %param.13) | copy-start | bytes 1156
  101.3 8.1 %copy-start.7 = (bf16[768,2048]{1,0:T(8,128)(2,1)S(1)}, bf16[768,2048]{1,0:T(8,128)(2,1)}, u32[]{:S(2)}) copy-start(bf16[768,2048]{1,0:T(8,128)(2,1)} %param.12) | copy-start | bytes 9437188
  247.8 64.9 %copy-start.9 = (f32[16,256,128]{2,1,0:T(8,128)S(1)}, f32[16,256,128]{2,1,0:T(8,128)}, u32[]{:S(2)}) copy-start(f32[16,256,128]{2,1,0:T(8,128)} %get-tuple-element.13) | copy-start | bytes 6291460
  312.7 7.5 %copy-start.8 = (bf16[768,2048]{1,0:T(8,128)(2,1)S(1)}, bf16[768,2048]{1,0:T(8,128)(2,1)}, u32[]{:S(2)}) copy-start(bf16[768,2048]{1,0:T(8,128)(2,1)} %param.12) | copy-start | bytes 9437188
  312.7 7.5 %copy-start.10 = (f32[16,256,128]{2,1,0:T(8,128)S(1)}, f32[16,256,128]{2,1,0:T(8,128)}, u32[]{:S(2)}) copy-start(f32[16,256,128]{2,1,0:T(8,128)} %get-tuple-element.13) | copy-start | bytes 6291460
  320.2 6.6 %copy-start.3 = (bf16[768,2048]{0,1:T(8,128)(2,1)S(1)}, bf16[768,2048]{0,1:T(8,128)(2,1)}, u32[]{:S(2)}) copy-start(bf16[768,2048]{0,1:T(8,128)(2,1)} %copy.30) | copy-start | bytes 9437188
  330.9 9.4 %copy-start.1 = (bf16[768,2048]{1,0:T(8,128)(2,1)S(1)}, bf16[768,2048]{1,0:T(8,128)(2,1)}, u32[]{:S(2)}) copy-start(bf16[768,2048]{1,0:T(8,128)(2,1)} %param.8) | copy-start | bytes 9437188
Sparse Core Ops, SparseCore 0:
  116.2 109.1 all-reduce.2
where the time goes:
time: 348 us; the launch traced here: 347 us
  blocking collectives  122 us (35%)
  waiting for transfers between devices  109 us (31%)
  matrix products  70.4 us (20%)
  local copies, waits for them, and re-layouts  28 us (8%)
  between operations  14.2 us (4%)
    psum x1, waiting for transfers between devices, per_device(): state, normalizer = lax.psum((partial_state, norm_part), 'seq')  109 us
    psum x1, blocking collectives, per_device(): state, normalizer = lax.psum((partial_state, norm_part), 'seq')  62.9 us
    psum x1, blocking collectives, per_device(): lax.psum((partial_gradient, norm_grad_part), 'seq')  59.4 us
    unnamed x33, local copies, waits for them, and re-layouts  24 us
    dot_general x1, matrix products, per_device(): jnp.einsum('thm,dm->thd', query_proj_grad, feature_matrix, preferred_elem...  8.75 us
    dot_general x1, matrix products, per_device(): jnp.einsum('nge,ngs->ges', query_random_features, scaled_block, preferred...  8.07 us
    dot_general x1, matrix products, per_device(): jnp.einsum('wkz,kzl->wkl', query_random_features, block_state, preferred_...  7.89 us
    dot_general x1, matrix products, per_device(): jnp.einsum('wkz,kzl->wkl', key_random_features, block_state_gradient, pre...  7.46 us
  transfers between devices with their start and end apart: 1, of which 1 were waited for; matrix products, arithmetic and copies ran while one was open for 0% of the time, Pallas kernels for 0%

commit v1 on v0

v1 whole, which is shorter than its diff:
```python
import functools

import jax
import jax.numpy as jnp
from jax import lax
from jax.experimental import pallas as pl
from jax.experimental.pallas import tpu as pltpu
from jax.sharding import PartitionSpec as P

F32 = jnp.float32
BF16 = jnp.bfloat16
ANY = pl.BlockSpec(memory_space=pl.ANY)
SMEM = pl.BlockSpec(memory_space=pltpu.SMEM)
VMEM = pl.BlockSpec(memory_space=pltpu.VMEM)
MESH = pl.DeviceIdType.MESH
VMEM_BYTES = 60 << 20
CHUNKS = 4


def dot(a, b, dims=((1,), (0,))):
    return lax.dot_general(a, b, (dims, ((), ())), preferred_element_type=F32)


class Reducer:
    def __init__(self, devices, rows, acc, landing, full, norm, norm_landing, sems):
        self.levels = devices.bit_length() - 1
        self.rows = rows
        self.acc, self.landing, self.full = acc, landing, full
        self.norm, self.norm_landing = norm, norm_landing
        self.send, self.recv, self.nsend, self.nrecv, self.gsend, self.grecv = sems
        self.me = lax.axis_index("seq")
        self.at = {}
        self.pending = {}
        self.sends = []

    def bit(self, chunk, level):
        order = list(range(self.levels))
        if chunk % CHUNKS == CHUNKS - 1 and self.levels > 2:
            order[1], order[2] = order[2], order[1]
        return 1 << order[level]

    def side(self, bit):
        return (self.me // bit) % 2

    def partner(self, bit):
        return self.me + bit - 2 * bit * self.side(bit)

    def greet(self):
        barrier = pltpu.get_barrier_semaphore()
        for level in range(self.levels):
            pl.semaphore_signal(
                barrier, inc=1, device_id={"seq": self.partner(1 << level)}, device_id_type=MESH
            )
        pl.semaphore_wait(barrier, self.levels)

    def offset(self, chunk, level):
        off = 0
        for s in range(level):
            off = off + self.side(self.bit(chunk, s)) * (self.rows >> (s + 1))
        return off

    def span(self, off, size):
        return pl.ds(pl.multiple_of(off, 8), size)

    def copy(self, src, dst, send, recv, bit):
        move = pltpu.make_async_remote_copy(
            src_ref=src, dst_ref=dst, send_sem=send, recv_sem=recv,
            device_id={"seq": self.partner(bit)}, device_id_type=MESH,
        )
        move.start()
        self.sends.append(move)
        return move

    def done(self, chunk):
        return self.at.get(chunk, 0) > 2 * self.levels

    def advance(self, chunk):
        step = self.at.get(chunk, 0)
        if step > 2 * self.levels:
            return
        levels = self.levels
        for move in self.pending.get(chunk, ()):
            move.wait_recv()
        if 1 <= step <= levels:
            last = step - 1
            half = self.rows >> step
            rows = self.span(self.offset(chunk, step), half)
            place = self.rows - (self.rows >> last)
            into = self.full if step == levels else self.acc
            into[chunk, rows, :] = (
                self.acc[chunk, rows, :] + self.landing[chunk, place : place + half, :]
            )
            self.norm[chunk, step] = self.norm[chunk, last] + self.norm_landing[chunk, last]
        if step < levels:
            bit = self.bit(chunk, step)
            half = self.rows >> (step + 1)
            away = self.offset(chunk, step) + (1 - self.side(bit)) * half
            place = self.rows - (self.rows >> step)
            self.pending[chunk] = (
                self.copy(
                    self.acc.at[chunk, self.span(away, half), :],
                    self.landing.at[chunk, place : place + half, :],
                    self.send.at[chunk, step], self.recv.at[chunk, step], bit,
                ),
                self.copy(
                    self.norm.at[chunk, step], self.norm_landing.at[chunk, step],
                    self.nsend.at[chunk, step], self.nrecv.at[chunk, step], bit,
                ),
            )
        elif step < 2 * levels:
            level = 2 * levels - step
            bit = self.bit(chunk, level - 1)
            rows = self.span(self.offset(chunk, level), self.rows >> level)
            self.pending[chunk] = (
                self.copy(
                    self.full.at[chunk, rows, :], self.full.at[chunk, rows, :],
                    self.gsend.at[chunk, level - 1], self.grecv.at[chunk, level - 1], bit,
                ),
            )
        self.at[chunk] = step + 1

    def finish(self):
        while not all(self.done(chunk) for chunk in range(CHUNKS)):
            for chunk in range(CHUNKS):
                self.advance(chunk)
        for move in self.sends:
            move.wait_send()


def reducer_scratch(devices, heads, features, width):
    levels = devices.bit_length() - 1
    rows = heads * features // CHUNKS
    dma = pltpu.SemaphoreType.DMA((CHUNKS, levels))
    return [
        pltpu.VMEM((CHUNKS, rows, width), F32),
        pltpu.VMEM((CHUNKS, rows, width), F32),
        pltpu.VMEM((CHUNKS, rows, width), F32),
        pltpu.VMEM((CHUNKS, levels + 1, heads // CHUNKS, features), F32),
        pltpu.VMEM((CHUNKS, levels, heads // CHUNKS, features), F32),
    ] + [dma] * 6


def key_kernel(
    devices, heads, blocks,
    k_hbm, v_hbm, q_hbm, ks, vs, qs, w,
    state_out, norm_out, kphi_out, qphi_out,
    kbuf, vbuf, qbuf, vb, kphi, qphi,
    acc, landing, full, norm, norm_landing, s0, s1, s2, s3, s4, s5, in_sem, out_sem,
):
    width, features = w.shape
    count = kbuf.shape[0]
    block = count // blocks
    per = heads // CHUNKS
    root_four, root_two = width**0.25, width**0.5
    loads = []
    for group, (src, dst) in enumerate(((k_hbm, kbuf), (v_hbm, vbuf), (q_hbm, qbuf))):
        loads.append([])
        for c in range(CHUNKS):
            cols = slice(c * per * width, (c + 1) * per * width)
            loads[group].append(
                pltpu.make_async_copy(src.at[:, cols], dst.at[:, cols], in_sem.at[group, c])
            )
    for c in range(CHUNKS):
        loads[0][c].start()
        loads[1][c].start()
    for c in range(CHUNKS):
        loads[2][c].start()
    red = Reducer(
        devices, per * features, acc, landing, full, norm, norm_landing, (s0, s1, s2, s3, s4, s5)
    )
    red.greet()
    stores = []

    def key_head(c, i, _):
        h = c * per + i
        cols = pl.ds(pl.multiple_of(h * width, width), width)
        proj = dot(kbuf[:, cols], w[...])
        total = jnp.zeros((1, features), F32)
        for b in range(blocks):
            rows = slice(b * block, (b + 1) * block)
            kf = kbuf[rows, cols].astype(F32) * ks[b, h]
            half_norm = jnp.sum(kf * kf, axis=1, keepdims=True) / (2.0 * root_two)
            phi = jnp.exp(proj[rows] * (ks[b, h] / root_four) - half_norm).astype(BF16)
            kphi[h, rows, :] = phi
            total = total + jnp.sum(phi.astype(F32), axis=0, keepdims=True)
            vb[rows, :] = (vbuf[rows, cols].astype(F32) * vs[b, h]).astype(BF16)
        acc[c, pl.ds(pl.multiple_of(i * features, features), features), :] = dot(
            kphi[h], vb[...], ((0,), (0,))
        )
        norm[c, 0, pl.ds(i, 1), :] = total
        return 0

    def query_head(h, _):
        cols = pl.ds(pl.multiple_of(h * width, width), width)
        proj = dot(qbuf[:, cols], w[...])
        for b in range(blocks):
            rows = slice(b * block, (b + 1) * block)
            qphi[h, rows, :] = jnp.exp(proj[rows] * (qs[b, h] / root_four)).astype(BF16)
        return 0

    for c in range(CHUNKS):
        loads[0][c].wait()
        loads[1][c].wait()
        lax.fori_loop(0, per, functools.partial(key_head, c), 0)
        for before in range(c + 1):
            red.advance(before)
        some = slice(c * per, (c + 1) * per)
        stores.append(pltpu.make_async_copy(kphi.at[some], kphi_out.at[some], out_sem.at[0, c]))
        stores[-1].start()
    for c in range(CHUNKS):
        loads[2][c].wait()
        for part in range(2):
            start = c * per + part * per // 2
            lax.fori_loop(start, start + per // 2, query_head, 0)
            for chunk in range(CHUNKS):
                red.advance(chunk)
        some = slice(c * per, (c + 1) * per)
        stores.append(pltpu.make_async_copy(qphi.at[some], qphi_out.at[some], out_sem.at[1, c]))
        stores[-1].start()
    red.finish()
    for c in range(CHUNKS):
        state_out[c] = full[c]
        norm_out[c] = norm[c, red.levels]
    for store in stores:
        store.wait()


def query_kernel(
    devices, heads,
    qphi_hbm, cot_hbm, state, norm_in, w,
    grad_out, norm_grad_out, att_hbm, qg_hbm,
    qphi, cot, att, qg, scb, stb, coup,
    acc, landing, full, norm, norm_landing, s0, s1, s2, s3, s4, s5, in_sem, out_sem,
):
    width, features = w.shape
    per = heads // CHUNKS
    root_four = width**0.25
    loads, stores = [], []
    for c in range(CHUNKS):
        cols = slice(c * per * width, (c + 1) * per * width)
        some = slice(c * per, (c + 1) * per)
        loads.append((
            pltpu.make_async_copy(qphi_hbm.at[some], qphi.at[some], in_sem.at[0, c]),
            pltpu.make_async_copy(cot_hbm.at[:, cols], cot.at[:, cols], in_sem.at[1, c]),
        ))
        for move in loads[-1]:
            move.start()
    red = Reducer(
        devices, per * features, acc, landing, full, norm, norm_landing, (s0, s1, s2, s3, s4, s5)
    )
    red.greet()

    def forward_head(c, i, _):
        h = c * per + i
        cols = pl.ds(pl.multiple_of(h * width, width), width)
        rows = pl.ds(pl.multiple_of(i * features, features), features)
        n = norm_in[c, pl.ds(i, 1), :]
        total = jnp.sum(n, axis=1, keepdims=True)
        block_state = (state[c, rows, :] / total).astype(BF16)
        stb[c, rows, :] = block_state
        phi = qphi[h].astype(F32)
        numerator = dot(qphi[h], block_state)
        inverse = 1.0 / jnp.sum(phi * n, axis=1, keepdims=True)
        attended = numerator * (total * inverse)
        att[:, cols] = attended.astype(BF16)
        scaled = cot[:, cols].astype(F32) * inverse
        coupling = jnp.sum(scaled * attended, axis=1, keepdims=True)
        coup[h] = coupling
        scb[:, cols] = scaled.astype(BF16)
        acc[c, rows, :] = dot(qphi[h], scb[:, cols], ((0,), (0,)))
        norm[c, 0, pl.ds(i, 1), :] = -jnp.sum(coupling * phi, axis=0, keepdims=True)
        return 0

    def grad_head(c, i, _):
        h = c * per + i
        cols = pl.ds(pl.multiple_of(h * width, width), width)
        rows = pl.ds(pl.multiple_of(i * features, features), features)
        n = norm_in[c, pl.ds(i, 1), :]
        total = jnp.sum(n, axis=1, keepdims=True)
        phi_grad = total * dot(scb[:, cols], stb[c, rows, :], ((1,), (1,))) - coup[h] * n
        proj_grad = (phi_grad * qphi[h].astype(F32)).astype(BF16)
        qg[:, cols] = (dot(proj_grad, w[...], ((1,), (1,))) / root_four).astype(BF16)
        return 0

    for c in range(CHUNKS):
        for move in loads[c]:
            move.wait()
        lax.fori_loop(0, per, functools.partial(forward_head, c), 0)
        for before in range(c + 1):
            red.advance(before)
        cols = slice(c * per * width, (c + 1) * per * width)
        stores.append(pltpu.make_async_copy(att.at[:, cols], att_hbm.at[:, cols], out_sem.at[0, c]))
        stores[-1].start()
    for c in range(CHUNKS):
        for part in range(2):
            start = part * per // 2
            lax.fori_loop(start, start + per // 2, functools.partial(grad_head, c), 0)
            for chunk in range(CHUNKS):
                red.advance(chunk)
        cols = slice(c * per * width, (c + 1) * per * width)
        stores.append(pltpu.make_async_copy(qg.at[:, cols], qg_hbm.at[:, cols], out_sem.at[1, c]))
        stores[-1].start()
    red.finish()
    for c in range(CHUNKS):
        grad_out[c] = full[c]
        norm_grad_out[c] = norm[c, red.levels]
    for store in stores:
        store.wait()


def value_kernel(blocks, k, v, kphi, grad, norm_in, norm_grad, ks, vs, w, kg, vg, vb):
    h = pl.program_id(0)
    width = w.shape[0]
    block = k.shape[0] // blocks
    root_four, root_two = width**0.25, width**0.5
    total = jnp.sum(norm_in[pl.ds(h, 1), :], axis=1, keepdims=True)
    inverse = 1.0 / total
    block_grad = (grad[0] * total).astype(BF16)
    for b in range(blocks):
        rows = slice(b * block, (b + 1) * block)
        vb[rows, :] = (v[rows, :].astype(F32) * vs[b, h]).astype(BF16)
    proj_grad = (
        dot(vb[...], block_grad, ((1,), (1,))) * inverse + norm_grad[pl.ds(h, 1), :]
    ) * kphi[0].astype(F32)
    sums = jnp.sum(proj_grad, axis=1, keepdims=True) / root_two
    out = dot(proj_grad.astype(BF16), w[...], ((1,), (1,))) / root_four
    for b in range(blocks):
        rows = slice(b * block, (b + 1) * block)
        kf = k[rows, :].astype(F32) * ks[b, h]
        kg[rows, :] = (out[rows] - sums[rows] * kf).astype(BF16)
    vg[...] = (dot(kphi[0], block_grad) * inverse).astype(BF16)


def per_device(
    devices,
    query_vals, query_scale, key_vals, key_scale, value_vals, value_scale, feature_matrix, cotangent,
):
    count, flat = query_vals.shape
    blocks, heads = query_scale.shape
    width, features = feature_matrix.shape
    per = heads // CHUNKS
    shape = jax.ShapeDtypeStruct
    phi_shape = shape((heads, count, features), BF16)
    state_shape = shape((CHUNKS, per * features, width), F32)
    norm_shape = shape((CHUNKS, per, features), F32)
    flat_shape = shape((count, flat), BF16)
    flat_scratch = pltpu.VMEM((count, flat), BF16)
    phi_scratch = pltpu.VMEM((heads, count, features), BF16)
    shared = reducer_scratch(devices, heads, features, width)

    def params(number):
        return pltpu.CompilerParams(
            collective_id=number, has_side_effects=True, vmem_limit_bytes=VMEM_BYTES
        )

    state, normalizer, kphi, qphi = pl.pallas_call(
        functools.partial(key_kernel, devices, heads, blocks),
        out_shape=(state_shape, norm_shape, phi_shape, phi_shape),
        in_specs=[ANY, ANY, ANY, SMEM, SMEM, SMEM, VMEM],
        out_specs=(VMEM, VMEM, ANY, ANY),
        scratch_shapes=[
            flat_scratch, flat_scratch, flat_scratch, pltpu.VMEM((count, width), BF16),
            phi_scratch, phi_scratch, *shared,
            pltpu.SemaphoreType.DMA((3, CHUNKS)), pltpu.SemaphoreType.DMA((2, CHUNKS)),
        ],
        compiler_params=params(0),
        name="key_state",
    )(key_vals, value_vals, query_vals, key_scale, value_scale, query_scale, feature_matrix)

    state_grad, norm_grad, attended, query_grad = pl.pallas_call(
        functools.partial(query_kernel, devices, heads),
        out_shape=(state_shape, norm_shape, flat_shape, flat_shape),
        in_specs=[ANY, ANY, VMEM, VMEM, VMEM],
        out_specs=(VMEM, VMEM, ANY, ANY),
        scratch_shapes=[
            phi_scratch, flat_scratch, flat_scratch, flat_scratch, flat_scratch,
            pltpu.VMEM((CHUNKS, per * features, width), BF16),
            pltpu.VMEM((heads, count, 1), F32), *shared,
            pltpu.SemaphoreType.DMA((2, CHUNKS)), pltpu.SemaphoreType.DMA((2, CHUNKS)),
        ],
        compiler_params=params(1),
        name="query_grad",
    )(qphi, cotangent, state, normalizer, feature_matrix)

    column = pl.BlockSpec((count, width), lambda h: (0, h))
    whole = pl.BlockSpec((heads, features), lambda h: (0, 0))
    key_grad, value_grad = pl.pallas_call(
        functools.partial(value_kernel, blocks),
        grid=(heads,),
        out_shape=(flat_shape, flat_shape),
        in_specs=[
            column, column,
            pl.BlockSpec((1, count, features), lambda h: (h, 0, 0)),
            pl.BlockSpec((1, features, width), lambda h: (h, 0, 0)),
            whole, whole, SMEM, SMEM,
            pl.BlockSpec((width, features), lambda h: (0, 0)),
        ],
        out_specs=(column, column),
        scratch_shapes=[pltpu.VMEM((count, width), BF16)],
        compiler_params=pltpu.CompilerParams(vmem_limit_bytes=VMEM_BYTES),
        name="key_grad",
    )(
        key_vals, value_vals, kphi, state_grad.reshape(heads, features, width),
        normalizer.reshape(heads, features), norm_grad.reshape(heads, features),
        key_scale, value_scale, feature_matrix,
    )
    return attended, query_grad, key_grad, value_grad


def solution(mesh):
    rows = P(("groups", "seq"), None)
    return jax.shard_map(
        functools.partial(per_device, mesh.shape["seq"]),
        mesh=mesh,
        in_specs=(rows, rows, rows, rows, rows, rows, P(), rows),
        out_specs=(rows, rows, rows, rows),
        check_vma=False,
    )
```

time: 348 us -> 135 us (0.39)
  Pallas kernels: 0 us -> 127 us
  blocking collectives: 122 us -> 0 us
  waiting for transfers between devices: 109 us -> 0 us
  matrix products: 70.4 us -> 0 us
  local copies, waits for them, and re-layouts: 28 us -> 6.64 us
  between operations: 14.2 us -> 0.67 us
    pallas_call x0 -> x3, Pallas kernels: none -> 127 us  [the longest x1 55.4 us: per_device(): pl.pallas_call(functools.partial(query_kernel, devices, heads), out_shape...]
    psum x2 -> x0, blocking collectives: 122 us -> none  [the longest x1 62.9 us: per_device(): state, normalizer = lax.psum((partial_state, norm_part), 'seq')]
    psum x1 -> x0, waiting for transfers between devices: 109 us -> none  [per_device(): state, normalizer = lax.psum((partial_state, norm_part), 'seq')]
    dot_general x11 -> x0, matrix products: 70.4 us -> none  [the longest x1 8.75 us: per_device(): jnp.einsum('thm,dm->thd', query_proj_grad, feature_matrix, preferred_elem...]
    unnamed x33 -> x8, local copies, waits for them, and re-layouts: 24 us -> 4.69 us
    convert_element_type x1 -> x0, local copies, waits for them, and re-layouts: 3.61 us -> none  [per_device(): scaled = upstream.astype(jnp.float32) / denominator[:, :, None]]
  transfers between devices with their start and end apart: 1 -> 0, of which waited for: 1 -> 0; matrix products, arithmetic and copies ran while one was open for 0% -> 0% of each run, Pallas kernels for 0% -> 0%
where the time goes in v1:
time: 135 us; the launch traced here: 134 us
  Pallas kernels  127 us (94%)
  local copies, waits for them, and re-layouts  6.64 us (5%)
    pallas_call x1, Pallas kernels, per_device(): pl.pallas_call(functools.partial(query_kernel, devices, heads), out_shape...  55.4 us
    pallas_call x1, Pallas kernels, per_device(): pl.pallas_call(functools.partial(key_kernel, devices, heads, blocks), out...  54.1 us
    pallas_call x1, Pallas kernels, per_device(): pl.pallas_call(functools.partial(value_kernel, blocks), grid=(heads,), ou...  17.2 us
    unnamed x8, local copies, waits for them, and re-layouts  4.69 us

profile of v1, /device:TPU:0, one launch (start us, length us, event | category | flops | bytes accessed | tf_op | source)
XLA Modules:
  0.0 134.0 jit_solution(9949503039248647862)
XLA Ops:
  0.6 54.1 %key_state.1 = (f32[4,1024,128]{2,1,0:T(8,128)}, f32[4,4,256]{2,1,0:T(4,128)}, bf16[16,768,256]{2,1,0:T(8,128)(2,1)}, bf16[16,768,256]{2,1,0:T(8,128)(2,1)}) custom-call(bf16[768,2048]{1,0:T(8,128)(2,1)} %k.1, bf16[768,2048]{1,0:T(8,128)(2,1)} %v.1, bf16[768,2048]{1,0:T(8,128)(2,1)} %q_hbm.1, f32[6,16]{1,0:T(8,128)} %ks.3, f32[6,16]{1,0:T(8,128)} %vs.3, ...), custom_call_target="tpu_custom_call" | custom-call | tf_op jit(solution)/shard_map/key_state/pallas_call | solution.py:356
  54.7 0.0 copy-start.2
  54.7 55.4 %query_grad.1 = (f32[4,1024,128]{2,1,0:T(8,128)}, f32[4,4,256]{2,1,0:T(4,128)}, bf16[768,2048]{1,0:T(8,128)(2,1)}, bf16[768,2048]{1,0:T(8,128)(2,1)}) custom-call(bf16[16,768,256]{2,1,0:T(8,128)(2,1)} %get-tuple-element.14.qphi_hbm, bf16[768,2048]{1,0:T(8,128)(2,1)} %cot_hbm.1, f32[4,1024,128]{2,1,0:T(8,128)} %get-tuple-element.15.state, ...), custom_call_target="tpu_custom_call" | custom-call | tf_op jit(solution)/shard_map/query_grad/pallas_call | solution.py:370
  110.1 1.3 reshape.19.norm_grad
  111.5 0.0 copy-done.2
  111.5 0.6 reshape.18.norm_in
  112.1 0.0 copy-start.1
  112.1 17.2 %key_grad.1 = (bf16[768,2048]{1,0:T(8,128)(2,1)}, bf16[768,2048]{1,0:T(8,128)(2,1)}) custom-call(bf16[768,2048]{1,0:T(8,128)(2,1)} %k.1, bf16[768,2048]{1,0:T(8,128)(2,1)} %v.1, bf16[16,768,256]{2,1,0:T(8,128)(2,1)} %get-tuple-element.19.kphi, f32[16,256,128]{2,1,0:T(8,128)} %bitcast.1, f32[16,256]{1,0:T(8,128)} %reshape.18.norm_in, ...), custom_call_target="tpu_custom_call" | custom-call | tf_op jit(solution)/shard_map/key_grad/pallas_call | solution.py:387
  129.3 0.0 copy-done.1
  129.3 0.0 copy-start
  129.3 1.7 %copy.14 = bf16[768,2048]{1,0:T(8,128)(2,1)} copy(bf16[768,2048]{1,0:T(8,128)(2,1)S(1)} %copy-done.1) | data formatting | bytes 6291456
  131.0 1.3 %copy-done = bf16[768,2048]{1,0:T(8,128)(2,1)S(1)} copy-done((bf16[768,2048]{1,0:T(8,128)(2,1)S(1)}, bf16[768,2048]{1,0:T(8,128)(2,1)}, u32[]{:S(2)}) %copy-start) | copy-done | bytes 3145752
  132.4 1.7 %copy.15 = bf16[768,2048]{1,0:T(8,128)(2,1)} copy(bf16[768,2048]{1,0:T(8,128)(2,1)S(1)} %copy-done) | data formatting | bytes 6291456
Async XLA Ops:
  54.7 56.8 %copy-start.2 = (f32[4,4,256]{2,1,0:T(4,128)S(1)}, f32[4,4,256]{2,1,0:T(4,128)}, u32[]{:S(2)}) copy-start(f32[4,4,256]{2,1,0:T(4,128)} %get-tuple-element.16.norm_in) | copy-start | bytes 49156
  112.1 17.2 %copy-start.1 = (bf16[768,2048]{1,0:T(8,128)(2,1)S(1)}, bf16[768,2048]{1,0:T(8,128)(2,1)}, u32[]{:S(2)}) copy-start(bf16[768,2048]{1,0:T(8,128)(2,1)} %get-tuple-element.28) | copy-start | bytes 9437188
  129.3 3.0 %copy-start = (bf16[768,2048]{1,0:T(8,128)(2,1)S(1)}, bf16[768,2048]{1,0:T(8,128)(2,1)}, u32[]{:S(2)}) copy-start(bf16[768,2048]{1,0:T(8,128)(2,1)} %get-tuple-element.29) | copy-start | bytes 9437188

commit v2 on v1

v2 whole, which is shorter than its diff:
```python
import functools

import jax
import jax.numpy as jnp
from jax import lax
from jax.experimental import pallas as pl
from jax.experimental.pallas import tpu as pltpu
from jax.sharding import PartitionSpec as P

F32 = jnp.float32
BF16 = jnp.bfloat16
ANY = pl.BlockSpec(memory_space=pl.ANY)
SMEM = pl.BlockSpec(memory_space=pltpu.SMEM)
VMEM = pl.BlockSpec(memory_space=pltpu.VMEM)
MESH = pl.DeviceIdType.MESH
VMEM_BYTES = 60 << 20
CHUNKS = 4
PAIR = 2
STEP_HEADS = 2


def dot(a, b, dims=((1,), (0,))):
    return lax.dot_general(a, b, (dims, ((), ())), preferred_element_type=F32)


def each_head(start, stop, body):
    def step(j, _):
        for k in range(PAIR):
            body(start + j * PAIR + k)
        return 0

    lax.fori_loop(0, (stop - start) // PAIR, step, 0)


class Reducer:
    def __init__(self, devices, rows, acc, landing, full, norm, norm_landing, sems):
        self.levels = devices.bit_length() - 1
        self.rows = rows
        self.acc, self.landing, self.full = acc, landing, full
        self.norm, self.norm_landing = norm, norm_landing
        self.send, self.recv, self.nsend, self.nrecv, self.gsend, self.grecv = sems
        self.me = lax.axis_index("seq")
        self.at = {}
        self.pending = {}
        self.sends = []

    def bit(self, chunk, level):
        order = list(range(self.levels))
        if chunk % 2 and self.levels > 2:
            order[1], order[2] = order[2], order[1]
        return 1 << order[level]

    def side(self, bit):
        return (self.me // bit) % 2

    def partner(self, bit):
        return self.me + bit - 2 * bit * self.side(bit)

    def greet(self):
        barrier = pltpu.get_barrier_semaphore()
        for level in range(self.levels):
            pl.semaphore_signal(
                barrier, inc=1, device_id={"seq": self.partner(1 << level)}, device_id_type=MESH
            )
        pl.semaphore_wait(barrier, self.levels)

    def offset(self, chunk, level):
        off = 0
        for s in range(level):
            off = off + self.side(self.bit(chunk, s)) * (self.rows >> (s + 1))
        return off

    def span(self, off, size):
        return pl.ds(pl.multiple_of(off, 8), size)

    def copy(self, src, dst, send, recv, bit):
        move = pltpu.make_async_remote_copy(
            src_ref=src, dst_ref=dst, send_sem=send, recv_sem=recv,
            device_id={"seq": self.partner(bit)}, device_id_type=MESH,
        )
        move.start()
        self.sends.append(move)
        return move

    def done(self, chunk):
        return self.at.get(chunk, 0) > 2 * self.levels

    def advance(self, chunk):
        step = self.at.get(chunk, 0)
        if step > 2 * self.levels:
            return
        levels = self.levels
        for move in self.pending.get(chunk, ()):
            move.wait_recv()
        if 1 <= step <= levels:
            last = step - 1
            half = self.rows >> step
            rows = self.span(self.offset(chunk, step), half)
            place = self.rows - (self.rows >> last)
            into = self.full if step == levels else self.acc
            into[chunk, rows, :] = (
                self.acc[chunk, rows, :] + self.landing[chunk, place : place + half, :]
            )
            self.norm[chunk, step] = self.norm[chunk, last] + self.norm_landing[chunk, last]
        if step < levels:
            bit = self.bit(chunk, step)
            half = self.rows >> (step + 1)
            away = self.offset(chunk, step) + (1 - self.side(bit)) * half
            place = self.rows - (self.rows >> step)
            self.pending[chunk] = (
                self.copy(
                    self.acc.at[chunk, self.span(away, half), :],
                    self.landing.at[chunk, place : place + half, :],
                    self.send.at[chunk, step], self.recv.at[chunk, step], bit,
                ),
                self.copy(
                    self.norm.at[chunk, step], self.norm_landing.at[chunk, step],
                    self.nsend.at[chunk, step], self.nrecv.at[chunk, step], bit,
                ),
            )
        elif step < 2 * levels:
            level = 2 * levels - step
            bit = self.bit(chunk, level - 1)
            rows = self.span(self.offset(chunk, level), self.rows >> level)
            self.pending[chunk] = (
                self.copy(
                    self.full.at[chunk, rows, :], self.full.at[chunk, rows, :],
                    self.gsend.at[chunk, level - 1], self.grecv.at[chunk, level - 1], bit,
                ),
            )
        self.at[chunk] = step + 1

    def finish(self):
        while not all(self.done(chunk) for chunk in range(CHUNKS)):
            for chunk in range(CHUNKS):
                self.advance(chunk)
        for move in self.sends:
            move.wait_send()


def reducer_scratch(devices, heads, features, width):
    levels = devices.bit_length() - 1
    rows = heads * features // CHUNKS
    dma = pltpu.SemaphoreType.DMA((CHUNKS, levels))
    return [
        pltpu.VMEM((CHUNKS, rows, width), F32),
        pltpu.VMEM((CHUNKS, rows, width), F32),
        pltpu.VMEM((CHUNKS, rows, width), F32),
        pltpu.VMEM((CHUNKS, levels + 1, heads // CHUNKS, features), F32),
        pltpu.VMEM((CHUNKS, levels, heads // CHUNKS, features), F32),
    ] + [dma] * 6


def main_kernel(
    devices, heads, blocks,
    k_hbm, v_hbm, q_hbm, cot_hbm, ks, vs, qs, w,
    norm_out, grad_out, norm_grad_out, kphi_out, att_hbm, qg_hbm,
    kbuf, vbuf, qbuf, vb, kphi, qphi, cot, scb, stb, coup, in_sem, out_sem, *shared,
):
    width, features = w.shape
    count = kbuf.shape[0]
    block = count // blocks
    per = heads // CHUNKS
    root_four, root_two = width**0.25, width**0.5
    att, qg = kbuf, vbuf
    spans = [slice(c * per * width, (c + 1) * per * width) for c in range(CHUNKS)]
    loads = []
    for group, (src, dst) in enumerate(
        ((k_hbm, kbuf), (v_hbm, vbuf), (q_hbm, qbuf), (cot_hbm, cot))
    ):
        loads.append([
            pltpu.make_async_copy(src.at[:, cols], dst.at[:, cols], in_sem.at[group, c])
            for c, cols in enumerate(spans)
        ])
    for c in range(CHUNKS):
        loads[0][c].start()
        loads[1][c].start()
    for c in range(CHUNKS):
        loads[2][c].start()
    for c in range(CHUNKS):
        loads[3][c].start()
    half = len(shared) // 2
    first = Reducer(devices, per * features, *shared[:5], shared[5:half])
    second = Reducer(devices, per * features, *shared[half : half + 5], shared[half + 5 :])
    first.greet()
    stores = []

    def key_head(c, i):
        h = c * per + i
        cols = pl.ds(pl.multiple_of(h * width, width), width)
        proj = dot(kbuf[:, cols], w[...])
        total = jnp.zeros((1, features), F32)
        for b in range(blocks):
            rows = slice(b * block, (b + 1) * block)
            kf = kbuf[rows, cols].astype(F32) * ks[b, h]
            half_norm = jnp.sum(kf * kf, axis=1, keepdims=True) / (2.0 * root_two)
            phi = jnp.exp(proj[rows] * (ks[b, h] / root_four) - half_norm).astype(BF16)
            kphi[h, rows, :] = phi
            total = total + jnp.sum(phi.astype(F32), axis=0, keepdims=True)
            vb[i % PAIR, rows, :] = (vbuf[rows, cols].astype(F32) * vs[b, h]).astype(BF16)
        first.acc[c, pl.ds(pl.multiple_of(i * features, features), features), :] = dot(
            kphi[h], vb[i % PAIR], ((0,), (0,))
        )
        first.norm[c, 0, pl.ds(i, 1), :] = total

    def query_head(h):
        cols = pl.ds(pl.multiple_of(h * width, width), width)
        proj = dot(qbuf[:, cols], w[...])
        for b in range(blocks):
            rows = slice(b * block, (b + 1) * block)
            qphi[h, rows, :] = jnp.exp(proj[rows] * (qs[b, h] / root_four)).astype(BF16)

    def forward_head(c, i):
        h = c * per + i
        cols = pl.ds(pl.multiple_of(h * width, width), width)
        rows = pl.ds(pl.multiple_of(i * features, features), features)
        n = first.norm[c, first.levels, pl.ds(i, 1), :]
        total = jnp.sum(n, axis=1, keepdims=True)
        block_state = (first.full[c, rows, :] / total).astype(BF16)
        stb[c, rows, :] = block_state
        phi = qphi[h].astype(F32)
        numerator = dot(qphi[h], block_state)
        inverse = 1.0 / jnp.sum(phi * n, axis=1, keepdims=True)
        attended = numerator * (total * inverse)
        att[:, cols] = attended.astype(BF16)
        scaled = cot[:, cols].astype(F32) * inverse
        coupling = jnp.sum(scaled * attended, axis=1, keepdims=True)
        coup[h] = coupling
        scb[:, cols] = scaled.astype(BF16)
        second.acc[c, rows, :] = dot(qphi[h], scb[:, cols], ((0,), (0,)))
        second.norm[c, 0, pl.ds(i, 1), :] = -jnp.sum(coupling * phi, axis=0, keepdims=True)

    def grad_head(c, i):
        h = c * per + i
        cols = pl.ds(pl.multiple_of(h * width, width), width)
        rows = pl.ds(pl.multiple_of(i * features, features), features)
        n = first.norm[c, first.levels, pl.ds(i, 1), :]
        total = jnp.sum(n, axis=1, keepdims=True)
        phi_grad = total * dot(scb[:, cols], stb[c, rows, :], ((1,), (1,))) - coup[h] * n
        proj_grad = (phi_grad * qphi[h].astype(F32)).astype(BF16)
        qg[:, cols] = (dot(proj_grad, w[...], ((1,), (1,))) / root_four).astype(BF16)

    def store(src, dst, group, c):
        stores.append(pltpu.make_async_copy(src, dst, out_sem.at[group, c]))
        stores[-1].start()

    forwarded = set()
    fillers = []
    for c in range(CHUNKS):
        for part in range(2):
            fillers.append((True, c, part))

    def fill():
        if not fillers:
            return
        early, c, part = fillers[0]
        if not early and c not in forwarded:
            return
        fillers.pop(0)
        start = part * per // 2
        if early:
            if part == 0:
                loads[2][c].wait()
            each_head(c * per + start, c * per + start + per // 2, query_head)
            return
        each_head(start, start + per // 2, functools.partial(grad_head, c))
        if part == 1:
            store(qg.at[:, spans[c]], qg_hbm.at[:, spans[c]], 2, c)

    def move(c):
        if not first.done(c):
            first.advance(c)
        elif c in forwarded:
            second.advance(c)
        elif not any(early and at == c for early, at, _ in fillers):
            loads[3][c].wait()
            each_head(0, per, functools.partial(forward_head, c))
            second.advance(c)
            store(att.at[:, spans[c]], att_hbm.at[:, spans[c]], 1, c)
            forwarded.add(c)
            fillers.extend((False, c, part) for part in range(2))

    for c in range(CHUNKS):
        loads[0][c].wait()
        loads[1][c].wait()
        each_head(0, per, functools.partial(key_head, c))
        for before in range(c + 1):
            first.advance(before)
        some = slice(c * per, (c + 1) * per)
        store(kphi.at[some], kphi_out.at[some], 0, c)
    while fillers or not all(second.done(c) for c in range(CHUNKS)):
        fill()
        for c in range(CHUNKS):
            move(c)
    first.finish()
    second.finish()
    for c in range(CHUNKS):
        norm_out[c] = first.norm[c, first.levels]
        grad_out[c] = second.full[c]
        norm_grad_out[c] = second.norm[c, second.levels]
    for each in stores:
        each.wait()


def value_kernel(blocks, k, v, kphi, grad, norm_in, norm_grad, ks, vs, w, kg, vg, vb):
    width = w.shape[0]
    per = norm_in.shape[1]
    block = k.shape[0] // blocks
    root_four, root_two = width**0.25, width**0.5
    for i in range(STEP_HEADS):
        h = pl.program_id(0) * STEP_HEADS + i
        cols = slice(i * width, (i + 1) * width)
        total = jnp.sum(norm_in[h // per, pl.ds(h % per, 1), :], axis=1, keepdims=True)
        inverse = 1.0 / total
        block_grad = (grad[i] * total).astype(BF16)
        for b in range(blocks):
            rows = slice(b * block, (b + 1) * block)
            vb[i, rows, :] = (v[rows, cols].astype(F32) * vs[b, h]).astype(BF16)
        proj_grad = (
            dot(vb[i], block_grad, ((1,), (1,))) * inverse
            + norm_grad[h // per, pl.ds(h % per, 1), :]
        ) * kphi[i].astype(F32)
        sums = jnp.sum(proj_grad, axis=1, keepdims=True) / root_two
        out = dot(proj_grad.astype(BF16), w[...], ((1,), (1,))) / root_four
        for b in range(blocks):
            rows = slice(b * block, (b + 1) * block)
            kf = k[rows, cols].astype(F32) * ks[b, h]
            kg[rows, cols] = (out[rows] - sums[rows] * kf).astype(BF16)
        vg[:, cols] = (dot(kphi[i], block_grad) * inverse).astype(BF16)


def per_device(
    devices,
    query_vals, query_scale, key_vals, key_scale, value_vals, value_scale, feature_matrix, cotangent,
):
    count, flat = query_vals.shape
    blocks, heads = query_scale.shape
    width, features = feature_matrix.shape
    per = heads // CHUNKS
    shape = jax.ShapeDtypeStruct
    phi_shape = shape((heads, count, features), BF16)
    state_shape = shape((CHUNKS, per * features, width), F32)
    norm_shape = shape((CHUNKS, per, features), F32)
    flat_shape = shape((count, flat), BF16)
    flat_scratch = pltpu.VMEM((count, flat), BF16)
    phi_scratch = pltpu.VMEM((heads, count, features), BF16)
    shared = reducer_scratch(devices, heads, features, width)

    normalizer, state_grad, norm_grad, kphi, attended, query_grad = pl.pallas_call(
        functools.partial(main_kernel, devices, heads, blocks),
        out_shape=(norm_shape, state_shape, norm_shape, phi_shape, flat_shape, flat_shape),
        in_specs=[ANY, ANY, ANY, ANY, SMEM, SMEM, SMEM, VMEM],
        out_specs=(VMEM, VMEM, VMEM, ANY, ANY, ANY),
        scratch_shapes=[
            flat_scratch, flat_scratch, flat_scratch, pltpu.VMEM((PAIR, count, width), BF16),
            phi_scratch, phi_scratch, flat_scratch, flat_scratch,
            pltpu.VMEM((CHUNKS, per * features, width), BF16),
            pltpu.VMEM((heads, count, 1), F32),
            pltpu.SemaphoreType.DMA((4, CHUNKS)), pltpu.SemaphoreType.DMA((3, CHUNKS)),
            *shared, *shared,
        ],
        compiler_params=pltpu.CompilerParams(
            collective_id=0, has_side_effects=True, vmem_limit_bytes=VMEM_BYTES
        ),
        name="attention",
    )(
        key_vals, value_vals, query_vals, cotangent, key_scale, value_scale, query_scale,
        feature_matrix,
    )

    column = pl.BlockSpec((count, STEP_HEADS * width), lambda h: (0, h))
    whole = pl.BlockSpec((CHUNKS, per, features), lambda h: (0, 0, 0))
    key_grad, value_grad = pl.pallas_call(
        functools.partial(value_kernel, blocks),
        grid=(heads // STEP_HEADS,),
        out_shape=(flat_shape, flat_shape),
        in_specs=[
            column, column,
            pl.BlockSpec((STEP_HEADS, count, features), lambda h: (h, 0, 0)),
            pl.BlockSpec((STEP_HEADS, features, width), lambda h: (h, 0, 0)),
            whole, whole, SMEM, SMEM,
            pl.BlockSpec((width, features), lambda h: (0, 0)),
        ],
        out_specs=(column, column),
        scratch_shapes=[pltpu.VMEM((STEP_HEADS, count, width), BF16)],
        compiler_params=pltpu.CompilerParams(vmem_limit_bytes=VMEM_BYTES),
        name="key_grad",
    )(
        key_vals, value_vals, kphi, state_grad.reshape(heads, features, width),
        normalizer, norm_grad,
        key_scale, value_scale, feature_matrix,
    )
    return attended, query_grad, key_grad, value_grad


def solution(mesh):
    rows = P(("groups", "seq"), None)
    return jax.shard_map(
        functools.partial(per_device, mesh.shape["seq"]),
        mesh=mesh,
        in_specs=(rows, rows, rows, rows, rows, rows, P(), rows),
        out_specs=(rows, rows, rows, rows),
        check_vma=False,
    )
```

time: 135 us -> 113 us (0.84)
  Pallas kernels: 127 us -> 106 us
  local copies, waits for them, and re-layouts: 6.64 us -> 4.69 us
    pallas_call x3 -> x2, Pallas kernels: 127 us -> 106 us  [the longest x1 93.4 us: per_device(): pl.pallas_call(functools.partial(main_kernel, devices, heads, blocks), ou...]
    reshape x2 -> x0, local copies, waits for them, and re-layouts: 1.95 us -> none  [the longest x1 1.33 us: per_device(): norm_grad.reshape(heads, features)]
    unnamed x8 -> x6, local copies, waits for them, and re-layouts: 4.69 us -> 4.69 us
where the time goes in v2:
time: 113 us; the launch traced here: 112 us
  Pallas kernels  106 us (94%)
  local copies, waits for them, and re-layouts  4.69 us (4%)
    pallas_call x1, Pallas kernels, per_device(): pl.pallas_call(functools.partial(main_kernel, devices, heads, blocks), ou...  93.4 us
    pallas_call x1, Pallas kernels, per_device(): pl.pallas_call(functools.partial(value_kernel, blocks), grid=(heads // ST...  12.9 us
    unnamed x6, local copies, waits for them, and re-layouts  4.69 us

profile of v2, /device:TPU:0, one launch (start us, length us, event | category | flops | bytes accessed | tf_op | source)
XLA Modules:
  0.0 111.6 jit_solution(6859028179209953798)
XLA Ops:
  0.6 93.4 %attention.1 = (f32[4,4,256]{2,1,0:T(4,128)}, f32[4,1024,128]{2,1,0:T(8,128)}, f32[4,4,256]{2,1,0:T(4,128)}, bf16[16,768,256]{2,1,0:T(8,128)(2,1)}, bf16[768,204...) custom-call(bf16[768,2048]{1,0:T(8,128)(2,1)} %k.1, bf16[768,2048]{1,0:T(8,128)(2,1)} %v.1, bf16[768,2048]{1,0:T(8,128)(2,1)} %q_hbm.1, ...), custom_call_target="tpu_custom_call" | custom-call | tf_op jit(solution)/shard_map/attention/pallas_call | solution.py:349
  94.0 0.0 copy-start.1
  94.0 12.9 %key_grad.1 = (bf16[768,2048]{1,0:T(8,128)(2,1)}, bf16[768,2048]{1,0:T(8,128)(2,1)}) custom-call(bf16[768,2048]{1,0:T(8,128)(2,1)} %k.1, bf16[768,2048]{1,0:T(8,128)(2,1)} %v.1, bf16[16,768,256]{2,1,0:T(8,128)(2,1)} %get-tuple-element.14.kphi, f32[16,256,128]{2,1,0:T(8,128)} %bitcast.1, f32[4,4,256]{2,1,0:T(4,128)} %get-tuple-element.16.norm_in, ...), custom_call_target="tpu_custom_call" | custom-call | tf_op jit(solution)/shard_map/key_grad/pallas_call | solution.py:373
  106.9 0.0 copy-done.1
  106.9 0.0 copy-start
  106.9 1.7 %copy.14 = bf16[768,2048]{1,0:T(8,128)(2,1)} copy(bf16[768,2048]{1,0:T(8,128)(2,1)S(1)} %copy-done.1) | data formatting | bytes 6291456
  108.6 1.3 %copy-done = bf16[768,2048]{1,0:T(8,128)(2,1)S(1)} copy-done((bf16[768,2048]{1,0:T(8,128)(2,1)S(1)}, bf16[768,2048]{1,0:T(8,128)(2,1)}, u32[]{:S(2)}) %copy-start) | copy-done | bytes 3145752
  109.9 1.7 %copy.15 = bf16[768,2048]{1,0:T(8,128)(2,1)} copy(bf16[768,2048]{1,0:T(8,128)(2,1)S(1)} %copy-done) | data formatting | bytes 6291456
Async XLA Ops:
  94.0 12.9 %copy-start.1 = (bf16[768,2048]{1,0:T(8,128)(2,1)S(1)}, bf16[768,2048]{1,0:T(8,128)(2,1)}, u32[]{:S(2)}) copy-start(bf16[768,2048]{1,0:T(8,128)(2,1)} %get-tuple-element.24) | copy-start | bytes 9437188
  106.9 3.0 %copy-start = (bf16[768,2048]{1,0:T(8,128)(2,1)S(1)}, bf16[768,2048]{1,0:T(8,128)(2,1)}, u32[]{:S(2)}) copy-start(bf16[768,2048]{1,0:T(8,128)(2,1)} %get-tuple-element.25) | copy-start | bytes 9437188
